TPU v7x, 256 devices: a whole 4x4x8 slice. The times are simulated.
256 devices in a mesh: sec: 4 (over y_lo, core), mom: 8 (over x, y_hi), en: 8 (over z).
Axes of the slice: x: 4, y: 4 (y_hi: 2, y_lo: 2; y = y_hi * 2 + y_lo), z: 8, core: 2. Of those that a mesh axis runs over, the one named last changes fastest.
Arguments:
- green_blocks: bfloat16 [8, 64, 2, 128, 128], P('mom', ('sec', 'en')), may hold values from -6 to 6
- derivative: bfloat16 [3, 128, 128], replicated, may hold values from -0.5 to 0.5
- bare_phonon: float32 [4, 8, 2, 3, 3, 128], P('sec', 'mom'), may hold values from -4 to 4
- prior_polar: float32 [4, 8, 2, 3, 3, 128], P('sec', 'mom'), may hold values from -4 to 4
- offsets: int32 [4], replicated, may hold values from 1 to 2, as said below
- momenta: int32 [8, 8], replicated, may hold values from 0 to 7, as said below
Outputs:
- sigma: float32 [8, 64, 2, 128, 128], P('mom', ('sec', 'en'))
- polarization: float32 [4, 8, 3, 128], P('sec', 'mom')
Inputs may be any that keep to these rules, and one draw needn't show every extreme that they name: `offsets`: every mode's offset lies in 1 to 2; some mode's offset equals 2 and another mode's equals 1. momenta[k, k'] = p((k - k') mod 8) for a permutation p of the 8 phonon momenta.
All inputs are finite; a program needn't handle non-finite values.
Results may differ from a plain program's by a relative error of at most 0.014.
Values may be sent and summed in bfloat16 or wider, within the bound.
No kernel may reach another device: no remote copies, remote signals or barrier semaphores. Data moves between devices by JAX's collectives and lax.ppermute only.
A program may use at most 64 MiB of HBM per device.

v0:
```python
import math
import jax
import jax.numpy as jnp
from jax import lax
from jax.sharding import PartitionSpec as P


def passed_along(x, axis, by):
    peers = lax.axis_size(axis)
    pairs = [(i, i + by) for i in range(peers) if 0 <= i + by < peers]
    return lax.ppermute(x, axis, pairs)


def contract(former, latter):
    return jnp.sum(former[..., :, :, None, :] * latter[..., None, :, :, :], axis=-3)


def complex_product(former, latter):
    real_part = contract(former[..., 0, :, :, :], latter[..., 0, :, :, :]) - contract(
        former[..., 1, :, :, :], latter[..., 1, :, :, :]
    )
    imag_part = contract(former[..., 0, :, :, :], latter[..., 1, :, :, :]) + contract(
        former[..., 1, :, :, :], latter[..., 0, :, :, :]
    )
    return jnp.stack([real_part, imag_part], axis=-4)


def dyson_update(bare_phonon, prior_polar):
    return bare_phonon + complex_product(complex_product(bare_phonon, prior_polar), bare_phonon)


def flipped_products(blocks, derivative):
    flipped = jnp.einsum(
        "ktcbx,ixa->kticab", blocks, derivative, preferred_element_type=jnp.float32
    )
    sign_flip = jnp.array([1.0, -1.0], jnp.float32).reshape(1, 1, 1, 2, 1, 1)
    return (flipped * sign_flip).astype(jnp.bfloat16)


def mode_weights(chosen):
    real_part = chosen[:, :, 0]
    imag_part = chosen[:, :, 1]
    upper_part = jnp.stack([real_part, -imag_part], axis=2)
    lower_part = jnp.stack([imag_part, real_part], axis=2)
    return jnp.stack([upper_part, lower_part], axis=2)


def weighted_rows(weights, selected):
    mode_count = weights.shape[1]
    total = None
    for mode_index in range(mode_count):
        for part_index in range(2):
            for direction in range(3):
                factor = jnp.transpose(
                    weights[:, mode_index, :, part_index, direction, :, :], (0, 2, 1, 3)
                )
                slab = selected[direction, :, mode_index, part_index].astype(jnp.float32)
                term = factor[:, None, :, :, :, None] * slab[None, :, None, None, :, :]
                total = term if total is None else total + term
    return total.astype(jnp.bfloat16)


def point_terms(source, chosen, derivative, offsets, targets, levels, flipped):
    blocks = jnp.einsum(
        "iab,scbd->iscad", derivative, source, preferred_element_type=jnp.float32
    ).astype(jnp.bfloat16)
    mode_count = chosen.shape[1]
    selected = jnp.stack(
        [
            lax.dynamic_slice_in_dim(blocks, levels - offsets[mode_index], targets, 1)
            for mode_index in range(mode_count)
        ],
        axis=2,
    )
    weights = mode_weights(chosen)
    combined = weighted_rows(weights, selected)
    sigma_part = jnp.einsum(
        "ktjxab,jbd->ktxad", combined, derivative, preferred_element_type=jnp.float32
    )
    polar_part = jnp.einsum(
        "itmcab,kticab->kmia", selected, flipped, preferred_element_type=jnp.float32
    )
    return (sigma_part, polar_part)


def per_device(green_blocks, derivative, bare_phonon, prior_polar, offsets, momenta):
    points = green_blocks.shape[0]
    levels = green_blocks.shape[1]
    block_order = green_blocks.shape[-1]
    all_points = points * lax.axis_size("mom")
    all_levels = levels * lax.axis_size("sec") * lax.axis_size("en")
    phonon = dyson_update(bare_phonon, prior_polar)
    local_modes = phonon.shape[0]
    stacked = phonon.reshape((local_modes * points,) + phonon.shape[2:])
    gathered = lax.all_gather(stacked, ("sec", "mom"), axis=0, tiled=True)
    mode_count = gathered.shape[0] // all_points
    phonon_table = jnp.transpose(
        gathered.reshape((mode_count, all_points) + phonon.shape[2:]), (1, 0, 2, 3, 4, 5)
    )
    own_rows = lax.dynamic_slice_in_dim(momenta, lax.axis_index("mom") * points, points, 0)
    momentum_ids = lax.broadcasted_iota(jnp.int32, (points, all_points), 1)
    lower_rim = passed_along(green_blocks, ("sec", "en"), 1)
    travelling = jnp.concatenate([lower_rim, green_blocks], axis=1)
    targets = green_blocks.shape[1]
    flipped = flipped_products(green_blocks, derivative)
    initial = (
        jnp.zeros((points, targets, 2, block_order, block_order), jnp.float32),
        jnp.zeros((all_points, mode_count, 3, block_order), jnp.float32),
    )
    pieces = lax.all_gather(travelling, "mom", axis=0, tiled=True)

    def one_point(position, running):
        sigma_sum, polar_sum = running
        source = lax.dynamic_index_in_dim(pieces, position, 0, keepdims=False)
        column = lax.dynamic_index_in_dim(own_rows, position, 1, keepdims=False)
        onehot = (column[:, None] == momentum_ids).astype(jnp.float32)
        chosen = jnp.einsum(
            "kq,qmxija->kmxija", onehot, phonon_table, precision=lax.Precision.HIGHEST
        )
        sigma_part, polar_part = point_terms(
            source, chosen, derivative, offsets, targets, levels, flipped
        )
        polar_sum = polar_sum + jnp.einsum(
            "kq,kmia->qmia", onehot, polar_part, precision=lax.Precision.HIGHEST
        )
        return (sigma_sum + sigma_part, polar_sum)

    sigma_sum, polar_sum = lax.fori_loop(0, pieces.shape[0], one_point, initial)
    sigma_scale = 1.0 / math.sqrt(9.0 * mode_count * all_points)
    polar_scale = 1.0 / math.sqrt(float(all_points * all_levels * block_order))
    ordered = jnp.transpose(polar_sum, (1, 0, 2, 3))
    summed = lax.psum(ordered, ("sec", "mom", "en"))
    own_share = lax.dynamic_slice(
        summed,
        (lax.axis_index("sec") * local_modes, lax.axis_index("mom") * points, 0, 0),
        (local_modes, points, 3, block_order),
    )
    return (sigma_sum * sigma_scale, own_share * polar_scale)


def solution(mesh):
    return jax.shard_map(
        per_device,
        mesh=mesh,
        in_specs=(
            P("mom", ("sec", "en"), None, None, None),
            P(),
            P("sec", "mom", None, None, None, None),
            P("sec", "mom", None, None, None, None),
            P(),
            P(),
        ),
        out_specs=(P("mom", ("sec", "en"), None, None, None), P("sec", "mom", None, None)),
        check_vma=False,
    )
```

profile of v0, /device:TPU:1, one launch (start us, length us, event | category | flops | bytes accessed | tf_op | source)
XLA Modules:
  0.0 422.1 jit_solution(5566107944990981499)
XLA Ops:
  7.3 4.5 %collective-permute-start = (bf16[1,2,2,128,128]{4,3,2,1,0:T(8,128)(2,1)}, bf16[1,2,2,128,128]{4,3,2,1,0:T(8,128)(2,1)S(1)}, u32[]{:S(2)}, u32[]{:S(2)}) collective-permute-start(bf16[1,2,2,128,128]{4,3,2,1,0:T(8,128)(2,1)} %param.9), channel_id=1, source_target_pairs={{0,1},{1,2},{2,3},{3,4},{4,5},{5,6},{6,7},{7,64},{64,65},{65,66},{... | collective-permute-start | bytes 393224 | tf_op jit(solution)/shard_map/ppermute | solution.py:11
  11.8 7.9 %collective-permute-done = bf16[1,2,2,128,128]{4,3,2,1,0:T(8,128)(2,1)S(1)} collective-permute-done((bf16[1,2,2,128,128]{4,3,2,1,0:T(8,128)(2,1)}, bf16[1,2,2,128,128]{4,3,2,1,0:T(8,128)(2,1)S(1)}, u32[]{:S(2)}, u32[]{:S(2)}) %collective-permute-start) | collective-permute-done | bytes 131104 | tf_op jit(solution)/shard_map/ppermute | solution.py:11
  19.7 1.6 pad_maximum_fusion.1
  21.3 1.5 fusion.141
  30.5 69.0 %all-gather = f32[32,1,2,3,3,128]{5,2,4,3,1,0:T(2,128)S(1)} all-gather(f32[1,1,2,3,3,128]{5,2,4,3,1,0:T(2,128)S(1)} %copy.131), channel_id=2, replica_groups=mesh['sec'=4,'mom'=8,'en'=8] {'sec','mom'}, dimensions={0}, use_global_device_ids=true | all-gather | bytes 304128 | tf_op jit(solution)/shard_map/all_gather | solution.py:95
  100.7 235.9 %while.19 = (s32[]{:T(128)}, f32[1,2,2,128,128]{4,3,2,1,0:T(8,128)}, f32[8,4,3,128]{3,2,1,0:T(4,128)}, s32[1,8]{1,0:T(1,128)}, f32[8,4,2,3,3,128]{5,4,3,2,1,0:T(...) while((s32[]{:T(128)}, ...), condition=%wide.region_9.10_spmd.clone, body=%wide.region_8.9_spmd.clone.sunk | while | flops 167619600 | bytes 31974176 | solution.py:128
  105.8 1.4 convolution_convert_fusion.2
  123.1 6.8 %fusion.167 = f32[1,2,2,128,128]{4,3,2,1,0:T(8,128)} fusion(f32[2,128,128]{2,1,0:T(8,128)S(1)} %copy-done.12, f32[3,2,128]{2,0,1:T(4,128)S(1)} %get-tuple-element.669, f32[2,128,128]{2,1,0:T(8,128)S(1)} %copy-done.13, f32[3,2,128]{2,0,1:T(4,128)S(1)} %get-tuple-element.671, f32[2,128,128]{2,1,0:T(8,128)} %copy.209, ...), kind=kOutput, calls=%fused_computation.5.clone.1 | convolution fusion | flops 59899904 | bytes 3842049 | tf_op jit(solution)/shard_map/while/body/eval_jaxpr/ktjxab,jbd->ktxad/dot_general | solution.py:77
  135.0 1.4 convolution_convert_fusion.2
  152.4 7.1 %fusion.167 = f32[1,2,2,128,128]{4,3,2,1,0:T(8,128)} fusion(f32[2,128,128]{2,1,0:T(8,128)S(1)} %copy-done.12, f32[3,2,128]{2,0,1:T(4,128)S(1)} %get-tuple-element.669, f32[2,128,128]{2,1,0:T(8,128)S(1)} %copy-done.13, f32[3,2,128]{2,0,1:T(4,128)S(1)} %get-tuple-element.671, f32[2,128,128]{2,1,0:T(8,128)} %copy.209, ...), kind=kOutput, calls=%fused_computation.5.clone.1 | convolution fusion | flops 59899904 | bytes 3842049 | tf_op jit(solution)/shard_map/while/body/eval_jaxpr/ktjxab,jbd->ktxad/dot_general | solution.py:77
  164.5 1.4 convolution_convert_fusion.2
  181.9 7.1 %fusion.167 = f32[1,2,2,128,128]{4,3,2,1,0:T(8,128)} fusion(f32[2,128,128]{2,1,0:T(8,128)S(1)} %copy-done.12, f32[3,2,128]{2,0,1:T(4,128)S(1)} %get-tuple-element.669, f32[2,128,128]{2,1,0:T(8,128)S(1)} %copy-done.13, f32[3,2,128]{2,0,1:T(4,128)S(1)} %get-tuple-element.671, f32[2,128,128]{2,1,0:T(8,128)} %copy.209, ...), kind=kOutput, calls=%fused_computation.5.clone.1 | convolution fusion | flops 59899904 | bytes 3842049 | tf_op jit(solution)/shard_map/while/body/eval_jaxpr/ktjxab,jbd->ktxad/dot_general | solution.py:77
  194.1 1.3 convolution_convert_fusion.2
  211.4 7.1 %fusion.167 = f32[1,2,2,128,128]{4,3,2,1,0:T(8,128)} fusion(f32[2,128,128]{2,1,0:T(8,128)S(1)} %copy-done.12, f32[3,2,128]{2,0,1:T(4,128)S(1)} %get-tuple-element.669, f32[2,128,128]{2,1,0:T(8,128)S(1)} %copy-done.13, f32[3,2,128]{2,0,1:T(4,128)S(1)} %get-tuple-element.671, f32[2,128,128]{2,1,0:T(8,128)} %copy.209, ...), kind=kOutput, calls=%fused_computation.5.clone.1 | convolution fusion | flops 59899904 | bytes 3842049 | tf_op jit(solution)/shard_map/while/body/eval_jaxpr/ktjxab,jbd->ktxad/dot_general | solution.py:77
  223.6 1.4 convolution_convert_fusion.2
  240.9 7.1 %fusion.167 = f32[1,2,2,128,128]{4,3,2,1,0:T(8,128)} fusion(f32[2,128,128]{2,1,0:T(8,128)S(1)} %copy-done.12, f32[3,2,128]{2,0,1:T(4,128)S(1)} %get-tuple-element.669, f32[2,128,128]{2,1,0:T(8,128)S(1)} %copy-done.13, f32[3,2,128]{2,0,1:T(4,128)S(1)} %get-tuple-element.671, f32[2,128,128]{2,1,0:T(8,128)} %copy.209, ...), kind=kOutput, calls=%fused_computation.5.clone.1 | convolution fusion | flops 59899904 | bytes 3842049 | tf_op jit(solution)/shard_map/while/body/eval_jaxpr/ktjxab,jbd->ktxad/dot_general | solution.py:77
  253.1 1.4 convolution_convert_fusion.2
  270.5 7.1 %fusion.167 = f32[1,2,2,128,128]{4,3,2,1,0:T(8,128)} fusion(f32[2,128,128]{2,1,0:T(8,128)S(1)} %copy-done.12, f32[3,2,128]{2,0,1:T(4,128)S(1)} %get-tuple-element.669, f32[2,128,128]{2,1,0:T(8,128)S(1)} %copy-done.13, f32[3,2,128]{2,0,1:T(4,128)S(1)} %get-tuple-element.671, f32[2,128,128]{2,1,0:T(8,128)} %copy.209, ...), kind=kOutput, calls=%fused_computation.5.clone.1 | convolution fusion | flops 59899904 | bytes 3842049 | tf_op jit(solution)/shard_map/while/body/eval_jaxpr/ktjxab,jbd->ktxad/dot_general | solution.py:77
  282.6 1.4 convolution_convert_fusion.2
  300.0 7.1 %fusion.167 = f32[1,2,2,128,128]{4,3,2,1,0:T(8,128)} fusion(f32[2,128,128]{2,1,0:T(8,128)S(1)} %copy-done.12, f32[3,2,128]{2,0,1:T(4,128)S(1)} %get-tuple-element.669, f32[2,128,128]{2,1,0:T(8,128)S(1)} %copy-done.13, f32[3,2,128]{2,0,1:T(4,128)S(1)} %get-tuple-element.671, f32[2,128,128]{2,1,0:T(8,128)} %copy.209, ...), kind=kOutput, calls=%fused_computation.5.clone.1 | convolution fusion | flops 59899904 | bytes 3842049 | tf_op jit(solution)/shard_map/while/body/eval_jaxpr/ktjxab,jbd->ktxad/dot_general | solution.py:77
  312.1 1.4 convolution_convert_fusion.2
  329.5 7.1 %fusion.167 = f32[1,2,2,128,128]{4,3,2,1,0:T(8,128)} fusion(f32[2,128,128]{2,1,0:T(8,128)S(1)} %copy-done.12, f32[3,2,128]{2,0,1:T(4,128)S(1)} %get-tuple-element.669, f32[2,128,128]{2,1,0:T(8,128)S(1)} %copy-done.13, f32[3,2,128]{2,0,1:T(4,128)S(1)} %get-tuple-element.671, f32[2,128,128]{2,1,0:T(8,128)} %copy.209, ...), kind=kOutput, calls=%fused_computation.5.clone.1 | convolution fusion | flops 59899904 | bytes 3842049 | tf_op jit(solution)/shard_map/while/body/eval_jaxpr/ktjxab,jbd->ktxad/dot_general | solution.py:77
  337.4 75.5 %psum.7 = f32[4,8,3,128]{3,1,2,0:T(8,128)S(1)} all-reduce(f32[4,8,3,128]{3,1,2,0:T(8,128)S(1)} %bitcast.412), channel_id=1, replica_groups=mesh['sec'=4,'mom'=8,'en'=8] {'sec','mom','en'}, use_global_device_ids=true, to_apply=%region_10.11 | all-reduce | flops 12288 | bytes 98304 | tf_op jit(solution)/shard_map/psum | solution.py:132
  413.0 1.7 broadcast_multiply_fusion
  (600 shorter events, 171.2 us)
Async XLA Ops:
  7.2 92.9 %copy-start = (s32[8,8]{1,0:T(8,128)S(1)}, s32[8,8]{1,0:T(8,128)}, u32[]{:S(2)}) copy-start(s32[8,8]{1,0:T(8,128)} %param.14) | copy-start | bytes 772
  7.2 92.5 %copy-start.18 = (f32[2]{0:T(128)S(1)}, f32[2]{0:T(128)}, u32[]{:S(2)}) copy-start(f32[2]{0:T(128)} %constant.97.clone) | copy-start | bytes 28
  7.2 92.5 %copy-start.16 = (bf16[1,2,2,128,128]{4,3,2,1,0:T(8,128)(2,1)S(1)}, bf16[1,2,2,128,128]{4,3,2,1,0:T(8,128)(2,1)}, u32[]{:S(2)}) copy-start(bf16[1,2,2,128,128]{4,3,2,1,0:T(8,128)(2,1)} %param.9) | copy-start | bytes 393220
  7.2 92.5 %copy-start.1 = (bf16[3,128,128]{2,1,0:T(8,128)(2,1)S(1)}, bf16[3,128,128]{2,1,0:T(8,128)(2,1)}, u32[]{:S(2)}) copy-start(bf16[3,128,128]{2,1,0:T(8,128)(2,1)} %param.10) | copy-start | bytes 294916
  7.2 93.5 %all-gather.3.cloned.1.call-start = ((), (), s32[]{:S(2)}) async-start(), calls=%async_computation | async-start | bytes 2359296 | tf_op jit(solution)/shard_map/all_gather | solution.py:110
  7.3 12.4 %collective-permute-start = (bf16[1,2,2,128,128]{4,3,2,1,0:T(8,128)(2,1)}, bf16[1,2,2,128,128]{4,3,2,1,0:T(8,128)(2,1)S(1)}, u32[]{:S(2)}, u32[]{:S(2)}) collective-permute-start(bf16[1,2,2,128,128]{4,3,2,1,0:T(8,128)(2,1)} %param.9), channel_id=1, source_target_pairs={{0,1},{1,2},{2,3},{3,4},{4,5},{5,6},{6,7},{7,64},{64,65},{65,66},{... | collective-permute-start | bytes 393224 | tf_op jit(solution)/shard_map/ppermute | solution.py:11
  117.1 5.9 %copy-start.2 = (f32[2,128,128]{2,1,0:T(8,128)S(1)}, f32[2,128,128]{2,1,0:T(8,128)}, u32[]{:S(2)}) copy-start(f32[2,128,128]{2,1,0:T(8,128)} %copy.221) | copy-start | bytes 393220 | tf_op jit(solution)/shard_map/while
  117.2 5.9 %copy-start.3 = (f32[2,128,128]{2,1,0:T(8,128)S(1)}, f32[2,128,128]{2,1,0:T(8,128)}, u32[]{:S(2)}) copy-start(f32[2,128,128]{2,1,0:T(8,128)} %copy.222) | copy-start | bytes 393220 | tf_op jit(solution)/shard_map/while
  117.2 5.9 %copy-start.4 = (f32[2,128,128]{2,1,0:T(8,128)S(1)}, f32[2,128,128]{2,1,0:T(8,128)}, u32[]{:S(2)}) copy-start(f32[2,128,128]{2,1,0:T(8,128)} %copy.223) | copy-start | bytes 393220 | tf_op jit(solution)/shard_map/while
  117.2 5.9 %copy-start.5 = (f32[2,128,128]{2,1,0:T(8,128)S(1)}, f32[2,128,128]{2,1,0:T(8,128)}, u32[]{:S(2)}) copy-start(f32[2,128,128]{2,1,0:T(8,128)} %copy.224) | copy-start | bytes 393220 | tf_op jit(solution)/shard_map/while
  117.2 5.9 %copy-start.6 = (f32[2,128,128]{2,1,0:T(8,128)S(1)}, f32[2,128,128]{2,1,0:T(8,128)}, u32[]{:S(2)}) copy-start(f32[2,128,128]{2,1,0:T(8,128)} %copy.225) | copy-start | bytes 393220 | tf_op jit(solution)/shard_map/while
  117.2 5.9 %copy-start.7 = (f32[2,128,128]{2,1,0:T(8,128)S(1)}, f32[2,128,128]{2,1,0:T(8,128)}, u32[]{:S(2)}) copy-start(f32[2,128,128]{2,1,0:T(8,128)} %copy.226) | copy-start | bytes 393220 | tf_op jit(solution)/shard_map/while
  146.4 5.9 %copy-start.2 = (f32[2,128,128]{2,1,0:T(8,128)S(1)}, f32[2,128,128]{2,1,0:T(8,128)}, u32[]{:S(2)}) copy-start(f32[2,128,128]{2,1,0:T(8,128)} %copy.221) | copy-start | bytes 393220 | tf_op jit(solution)/shard_map/while
  146.4 5.9 %copy-start.3 = (f32[2,128,128]{2,1,0:T(8,128)S(1)}, f32[2,128,128]{2,1,0:T(8,128)}, u32[]{:S(2)}) copy-start(f32[2,128,128]{2,1,0:T(8,128)} %copy.222) | copy-start | bytes 393220 | tf_op jit(solution)/shard_map/while
  146.4 5.9 %copy-start.4 = (f32[2,128,128]{2,1,0:T(8,128)S(1)}, f32[2,128,128]{2,1,0:T(8,128)}, u32[]{:S(2)}) copy-start(f32[2,128,128]{2,1,0:T(8,128)} %copy.223) | copy-start | bytes 393220 | tf_op jit(solution)/shard_map/while
  146.4 5.9 %copy-start.5 = (f32[2,128,128]{2,1,0:T(8,128)S(1)}, f32[2,128,128]{2,1,0:T(8,128)}, u32[]{:S(2)}) copy-start(f32[2,128,128]{2,1,0:T(8,128)} %copy.224) | copy-start | bytes 393220 | tf_op jit(solution)/shard_map/while
  146.4 5.9 %copy-start.6 = (f32[2,128,128]{2,1,0:T(8,128)S(1)}, f32[2,128,128]{2,1,0:T(8,128)}, u32[]{:S(2)}) copy-start(f32[2,128,128]{2,1,0:T(8,128)} %copy.225) | copy-start | bytes 393220 | tf_op jit(solution)/shard_map/while
  146.4 5.9 %copy-start.7 = (f32[2,128,128]{2,1,0:T(8,128)S(1)}, f32[2,128,128]{2,1,0:T(8,128)}, u32[]{:S(2)}) copy-start(f32[2,128,128]{2,1,0:T(8,128)} %copy.226) | copy-start | bytes 393220 | tf_op jit(solution)/shard_map/while
  175.9 5.9 %copy-start.2 = (f32[2,128,128]{2,1,0:T(8,128)S(1)}, f32[2,128,128]{2,1,0:T(8,128)}, u32[]{:S(2)}) copy-start(f32[2,128,128]{2,1,0:T(8,128)} %copy.221) | copy-start | bytes 393220 | tf_op jit(solution)/shard_map/while
  175.9 5.9 %copy-start.3 = (f32[2,128,128]{2,1,0:T(8,128)S(1)}, f32[2,128,128]{2,1,0:T(8,128)}, u32[]{:S(2)}) copy-start(f32[2,128,128]{2,1,0:T(8,128)} %copy.222) | copy-start | bytes 393220 | tf_op jit(solution)/shard_map/while
  175.9 5.9 %copy-start.4 = (f32[2,128,128]{2,1,0:T(8,128)S(1)}, f32[2,128,128]{2,1,0:T(8,128)}, u32[]{:S(2)}) copy-start(f32[2,128,128]{2,1,0:T(8,128)} %copy.223) | copy-start | bytes 393220 | tf_op jit(solution)/shard_map/while
  175.9 5.9 %copy-start.5 = (f32[2,128,128]{2,1,0:T(8,128)S(1)}, f32[2,128,128]{2,1,0:T(8,128)}, u32[]{:S(2)}) copy-start(f32[2,128,128]{2,1,0:T(8,128)} %copy.224) | copy-start | bytes 393220 | tf_op jit(solution)/shard_map/while
  175.9 5.9 %copy-start.6 = (f32[2,128,128]{2,1,0:T(8,128)S(1)}, f32[2,128,128]{2,1,0:T(8,128)}, u32[]{:S(2)}) copy-start(f32[2,128,128]{2,1,0:T(8,128)} %copy.225) | copy-start | bytes 393220 | tf_op jit(solution)/shard_map/while
  176.0 5.9 %copy-start.7 = (f32[2,128,128]{2,1,0:T(8,128)S(1)}, f32[2,128,128]{2,1,0:T(8,128)}, u32[]{:S(2)}) copy-start(f32[2,128,128]{2,1,0:T(8,128)} %copy.226) | copy-start | bytes 393220 | tf_op jit(solution)/shard_map/while
  (102 other events, 350.4 us)
Sparse Core Ops, SparseCore 0:
  21.4 60.3 all-gather.2
where the time goes:
time: 428 us; the launch traced here: 422 us
  blocking collectives  145 us (34%)
  local copies, waits for them, and re-layouts  135 us (32%)
  matrix products  76.3 us (18%)
  other arithmetic  31.9 us (7%)
  between operations  19.4 us (5%)
  waiting for transfers between devices  7.91 us (2%)
  starting transfers between devices  4.53 us (1%)
    mul x192, local copies, waits for them, and re-layouts, weighted_rows(): term = factor[:, None, :, :, :, None] * slab[None, :, None, None, :, :]  108 us
    psum x1, blocking collectives, per_device(): summed = lax.psum(ordered, ('sec', 'mom', 'en'))  75.5 us
    all_gather x1, blocking collectives, per_device(): gathered = lax.all_gather(stacked, ('sec', 'mom'), axis=0, tiled=True)  69 us
    dot_general x8, matrix products, point_terms(): jnp.einsum('ktjxab,jbd->ktxad', combined, derivative, preferred_element_t...  56.2 us
    mul x40, other arithmetic, weighted_rows(): term = factor[:, None, :, :, :, None] * slab[None, :, None, None, :, :]  12.7 us
    dot_general x8, matrix products, point_terms(): jnp.einsum('iab,scbd->iscad', derivative, source, preferred_element_type=...  10.8 us
    dynamic_slice x8, local copies, waits for them, and re-layouts, one_point(): column = lax.dynamic_index_in_dim(own_rows, position, 1, keepdims=False)  10.7 us
    another operation x8, other arithmetic  10.2 us
  transfers between devices with their start and end apart: 2, of which 1 were waited for; matrix products, arithmetic and copies ran while one was open for 1% of the time, Pallas kernels for 0%

commit v1 on v0

--- a/solution.py
+++ b/solution.py
@@ -92,7 +92,10 @@
     phonon = dyson_update(bare_phonon, prior_polar)
     local_modes = phonon.shape[0]
     stacked = phonon.reshape((local_modes * points,) + phonon.shape[2:])
-    gathered = lax.all_gather(stacked, ("sec", "mom"), axis=0, tiled=True)
+    r2 = lax.axis_size(("sec", "mom"))
+    u1 = jnp.stack([stacked] * r2, axis=0)
+    built = lax.all_to_all(u1, ("sec", "mom"), 0, 0)
+    gathered = jnp.concatenate(built, axis=0)
     mode_count = gathered.shape[0] // all_points
     phonon_table = jnp.transpose(
         gathered.reshape((mode_count, all_points) + phonon.shape[2:]), (1, 0, 2, 3, 4, 5)

time: 428 us -> 406 us (0.949)
  blocking collectives: 145 us -> 77.3 us
  waiting for transfers between devices: 7.91 us -> 49.3 us
  starting transfers between devices: 4.53 us -> 11.7 us
    all_gather x1 -> x0, blocking collectives: 69 us -> none  [per_device(): gathered = lax.all_gather(stacked, ('sec', 'mom'), axis=0, tiled=True)]
    all_gather x1, waiting for transfers between devices: 0.01 us -> 37.5 us  [per_device(): pieces = lax.all_gather(travelling, 'mom', axis=0, tiled=True)]
    all_to_all x0 -> x1, starting transfers between devices: none -> 7.2 us  [per_device(): built = lax.all_to_all(u1, ('sec', 'mom'), 0, 0)]
  transfers between devices with their start and end apart: 2 -> 3, of which waited for: 1 -> 3; matrix products, arithmetic and copies ran while one was open for 1% -> 1% of each run, Pallas kernels for 0% -> 0%
where the time goes in v1:
time: 406 us; the launch traced here: 400 us
  local copies, waits for them, and re-layouts  133 us (33%)
  blocking collectives  77.3 us (19%)
  matrix products  75.7 us (19%)
  waiting for transfers between devices  49.3 us (12%)
  other arithmetic  31.2 us (8%)
  between operations  19.4 us (5%)
  starting transfers between devices  11.7 us (3%)
    mul x192, local copies, waits for them, and re-layouts, weighted_rows(): term = factor[:, None, :, :, :, None] * slab[None, :, None, None, :, :]  107 us
    psum x1, blocking collectives, per_device(): summed = lax.psum(ordered, ('sec', 'mom', 'en'))  77.3 us
    dot_general x8, matrix products, point_terms(): jnp.einsum('ktjxab,jbd->ktxad', combined, derivative, preferred_element_t...  56.2 us
    all_gather x1, waiting for transfers between devices, per_device(): pieces = lax.all_gather(travelling, 'mom', axis=0, tiled=True)  37.5 us
    mul x40, other arithmetic, weighted_rows(): term = factor[:, None, :, :, :, None] * slab[None, :, None, None, :, :]  12.8 us
    dot_general x8, matrix products, point_terms(): jnp.einsum('iab,scbd->iscad', derivative, source, preferred_element_type=...  10.8 us
    dynamic_slice x8, local copies, waits for them, and re-layouts, one_point(): column = lax.dynamic_index_in_dim(own_rows, position, 1, keepdims=False)  10 us
    while x256, local copies, waits for them, and re-layouts  9.92 us
  transfers between devices with their start and end apart: 3, of which 3 were waited for; matrix products, arithmetic and copies ran while one was open for 1% of the time, Pallas kernels for 0%

profile of v1, /device:TPU:1, one launch (start us, length us, event | category | flops | bytes accessed | tf_op | source)
XLA Modules:
  0.0 400.3 jit_solution(10660584739055606494)
XLA Ops:
  7.3 4.5 %collective-permute-start = (bf16[1,2,2,128,128]{4,3,2,1,0:T(8,128)(2,1)}, bf16[1,2,2,128,128]{4,3,2,1,0:T(8,128)(2,1)S(1)}, u32[]{:S(2)}, u32[]{:S(2)}) collective-permute-start(bf16[1,2,2,128,128]{4,3,2,1,0:T(8,128)(2,1)} %param.9), channel_id=1, source_target_pairs={{0,1},{1,2},{2,3},{3,4},{4,5},{5,6},{6,7},{7,64},{64,65},{65,66},{... | collective-permute-start | bytes 393224 | tf_op jit(solution)/shard_map/ppermute | solution.py:11
  11.8 7.9 %collective-permute-done = bf16[1,2,2,128,128]{4,3,2,1,0:T(8,128)(2,1)S(1)} collective-permute-done((bf16[1,2,2,128,128]{4,3,2,1,0:T(8,128)(2,1)}, bf16[1,2,2,128,128]{4,3,2,1,0:T(8,128)(2,1)S(1)}, u32[]{:S(2)}, u32[]{:S(2)}) %collective-permute-start) | collective-permute-done | bytes 131104 | tf_op jit(solution)/shard_map/ppermute | solution.py:11
  19.7 1.6 pad_maximum_fusion.1
  24.7 7.2 %all-to-all-start = ((f32[32,1,2,3,3,128]{5,2,4,3,1,0:T(2,128)}), f32[32,1,2,3,3,128]{5,2,4,3,1,0:T(2,128)S(1)}, u32[]{:S(2)}, u32[]{:S(2)}) async-start(f32[32,1,2,3,3,128]{5,2,4,3,1,0:T(2,128)} %stack.112), calls=%async_computation | async-start | bytes 589824 | tf_op jit(solution)/shard_map/all_to_all | solution.py:97
  38.6 3.9 all-to-all-done
  42.8 37.5 %all-gather.2.cloned.1.call-done = bf16[8,4,2,128,128]{4,3,2,1,0:T(8,128)(2,1)} async-done(((bf16[1,4,2,128,128]{4,3,2,1,0:T(8,128)(2,1)}), bf16[8,4,2,128,128]{4,3,2,1,0:T(8,128)(2,1)}) %all-gather.2.cloned.1.call-update) | async-done | bytes 2097168 | tf_op jit(solution)/shard_map/all_gather | solution.py:113
  80.3 232.8 %while.19 = (s32[]{:T(128)}, f32[1,2,2,128,128]{4,3,2,1,0:T(8,128)}, f32[8,4,3,128]{3,2,1,0:T(4,128)}, s32[1,8]{1,0:T(1,128)}, f32[8,4,2,3,3,128]{5,4,3,2,1,0:T(...) while((s32[]{:T(128)}, ...), condition=%wide.region_9.10_spmd.clone, body=%wide.region_8.9_spmd.clone.sunk | while | flops 167619600 | bytes 31974176 | solution.py:131
  85.1 1.3 convolution_convert_fusion.2
  102.3 6.8 %fusion.168 = f32[1,2,2,128,128]{4,3,2,1,0:T(8,128)} fusion(f32[2,128,128]{2,1,0:T(8,128)S(1)} %copy-done.12, f32[3,2,128]{2,0,1:T(4,128)S(1)} %get-tuple-element.681, f32[2,128,128]{2,1,0:T(8,128)S(1)} %copy-done.13, f32[3,2,128]{2,0,1:T(4,128)S(1)} %get-tuple-element.683, f32[2,128,128]{2,1,0:T(8,128)} %copy.241, ...), kind=kOutput, calls=%fused_computation.5.clone.1 | convolution fusion | flops 59899904 | bytes 3842049 | tf_op jit(solution)/shard_map/while/body/eval_jaxpr/ktjxab,jbd->ktxad/dot_general | solution.py:77
  131.2 7.1 %fusion.168 = f32[1,2,2,128,128]{4,3,2,1,0:T(8,128)} fusion(f32[2,128,128]{2,1,0:T(8,128)S(1)} %copy-done.12, f32[3,2,128]{2,0,1:T(4,128)S(1)} %get-tuple-element.681, f32[2,128,128]{2,1,0:T(8,128)S(1)} %copy-done.13, f32[3,2,128]{2,0,1:T(4,128)S(1)} %get-tuple-element.683, f32[2,128,128]{2,1,0:T(8,128)} %copy.241, ...), kind=kOutput, calls=%fused_computation.5.clone.1 | convolution fusion | flops 59899904 | bytes 3842049 | tf_op jit(solution)/shard_map/while/body/eval_jaxpr/ktjxab,jbd->ktxad/dot_general | solution.py:77
  143.1 1.3 convolution_convert_fusion.2
  160.3 7.1 %fusion.168 = f32[1,2,2,128,128]{4,3,2,1,0:T(8,128)} fusion(f32[2,128,128]{2,1,0:T(8,128)S(1)} %copy-done.12, f32[3,2,128]{2,0,1:T(4,128)S(1)} %get-tuple-element.681, f32[2,128,128]{2,1,0:T(8,128)S(1)} %copy-done.13, f32[3,2,128]{2,0,1:T(4,128)S(1)} %get-tuple-element.683, f32[2,128,128]{2,1,0:T(8,128)} %copy.241, ...), kind=kOutput, calls=%fused_computation.5.clone.1 | convolution fusion | flops 59899904 | bytes 3842049 | tf_op jit(solution)/shard_map/while/body/eval_jaxpr/ktjxab,jbd->ktxad/dot_general | solution.py:77
  172.3 1.3 convolution_convert_fusion.2
  189.5 7.1 %fusion.168 = f32[1,2,2,128,128]{4,3,2,1,0:T(8,128)} fusion(f32[2,128,128]{2,1,0:T(8,128)S(1)} %copy-done.12, f32[3,2,128]{2,0,1:T(4,128)S(1)} %get-tuple-element.681, f32[2,128,128]{2,1,0:T(8,128)S(1)} %copy-done.13, f32[3,2,128]{2,0,1:T(4,128)S(1)} %get-tuple-element.683, f32[2,128,128]{2,1,0:T(8,128)} %copy.241, ...), kind=kOutput, calls=%fused_computation.5.clone.1 | convolution fusion | flops 59899904 | bytes 3842049 | tf_op jit(solution)/shard_map/while/body/eval_jaxpr/ktjxab,jbd->ktxad/dot_general | solution.py:77
  201.4 1.4 convolution_convert_fusion.2
  218.6 7.1 %fusion.168 = f32[1,2,2,128,128]{4,3,2,1,0:T(8,128)} fusion(f32[2,128,128]{2,1,0:T(8,128)S(1)} %copy-done.12, f32[3,2,128]{2,0,1:T(4,128)S(1)} %get-tuple-element.681, f32[2,128,128]{2,1,0:T(8,128)S(1)} %copy-done.13, f32[3,2,128]{2,0,1:T(4,128)S(1)} %get-tuple-element.683, f32[2,128,128]{2,1,0:T(8,128)} %copy.241, ...), kind=kOutput, calls=%fused_computation.5.clone.1 | convolution fusion | flops 59899904 | bytes 3842049 | tf_op jit(solution)/shard_map/while/body/eval_jaxpr/ktjxab,jbd->ktxad/dot_general | solution.py:77
  230.5 1.3 convolution_convert_fusion.2
  247.8 7.1 %fusion.168 = f32[1,2,2,128,128]{4,3,2,1,0:T(8,128)} fusion(f32[2,128,128]{2,1,0:T(8,128)S(1)} %copy-done.12, f32[3,2,128]{2,0,1:T(4,128)S(1)} %get-tuple-element.681, f32[2,128,128]{2,1,0:T(8,128)S(1)} %copy-done.13, f32[3,2,128]{2,0,1:T(4,128)S(1)} %get-tuple-element.683, f32[2,128,128]{2,1,0:T(8,128)} %copy.241, ...), kind=kOutput, calls=%fused_computation.5.clone.1 | convolution fusion | flops 59899904 | bytes 3842049 | tf_op jit(solution)/shard_map/while/body/eval_jaxpr/ktjxab,jbd->ktxad/dot_general | solution.py:77
  259.7 1.3 convolution_convert_fusion.2
  276.9 7.1 %fusion.168 = f32[1,2,2,128,128]{4,3,2,1,0:T(8,128)} fusion(f32[2,128,128]{2,1,0:T(8,128)S(1)} %copy-done.12, f32[3,2,128]{2,0,1:T(4,128)S(1)} %get-tuple-element.681, f32[2,128,128]{2,1,0:T(8,128)S(1)} %copy-done.13, f32[3,2,128]{2,0,1:T(4,128)S(1)} %get-tuple-element.683, f32[2,128,128]{2,1,0:T(8,128)} %copy.241, ...), kind=kOutput, calls=%fused_computation.5.clone.1 | convolution fusion | flops 59899904 | bytes 3842049 | tf_op jit(solution)/shard_map/while/body/eval_jaxpr/ktjxab,jbd->ktxad/dot_general | solution.py:77
  288.8 1.4 convolution_convert_fusion.2
  306.0 7.1 %fusion.168 = f32[1,2,2,128,128]{4,3,2,1,0:T(8,128)} fusion(f32[2,128,128]{2,1,0:T(8,128)S(1)} %copy-done.12, f32[3,2,128]{2,0,1:T(4,128)S(1)} %get-tuple-element.681, f32[2,128,128]{2,1,0:T(8,128)S(1)} %copy-done.13, f32[3,2,128]{2,0,1:T(4,128)S(1)} %get-tuple-element.683, f32[2,128,128]{2,1,0:T(8,128)} %copy.241, ...), kind=kOutput, calls=%fused_computation.5.clone.1 | convolution fusion | flops 59899904 | bytes 3842049 | tf_op jit(solution)/shard_map/while/body/eval_jaxpr/ktjxab,jbd->ktxad/dot_general | solution.py:77
  314.0 77.3 %psum.7 = f32[4,8,3,128]{3,1,2,0:T(8,128)S(1)} all-reduce(f32[4,8,3,128]{3,1,2,0:T(8,128)S(1)} %bitcast.414), channel_id=1, replica_groups=mesh['sec'=4,'mom'=8,'en'=8] {'sec','mom','en'}, use_global_device_ids=true, to_apply=%region_10.11 | all-reduce | flops 12288 | bytes 98304 | tf_op jit(solution)/shard_map/psum | solution.py:135
  391.3 1.7 broadcast_multiply_fusion
  (604 shorter events, 171.0 us)
Async XLA Ops:
  7.2 30.9 %copy-start = (s32[8,8]{1,0:T(8,128)S(1)}, s32[8,8]{1,0:T(8,128)}, u32[]{:S(2)}) copy-start(s32[8,8]{1,0:T(8,128)} %param.14) | copy-start | bytes 772
  7.2 30.5 %copy-start.19 = (f32[2]{0:T(128)S(1)}, f32[2]{0:T(128)}, u32[]{:S(2)}) copy-start(f32[2]{0:T(128)} %constant.97.clone) | copy-start | bytes 28
  7.2 30.5 %copy-start.16 = (bf16[1,2,2,128,128]{4,3,2,1,0:T(8,128)(2,1)S(1)}, bf16[1,2,2,128,128]{4,3,2,1,0:T(8,128)(2,1)}, u32[]{:S(2)}) copy-start(bf16[1,2,2,128,128]{4,3,2,1,0:T(8,128)(2,1)} %param.9) | copy-start | bytes 393220
  7.2 24.7 %copy-start.18 = (s32[4]{0:T(128)S(1)}, s32[4]{0:T(128)}, u32[]{:S(2)}) copy-start(s32[4]{0:T(128)} %param.13) | copy-start | bytes 52
  7.2 30.5 %copy-start.1 = (bf16[3,128,128]{2,1,0:T(8,128)(2,1)S(1)}, bf16[3,128,128]{2,1,0:T(8,128)(2,1)}, u32[]{:S(2)}) copy-start(bf16[3,128,128]{2,1,0:T(8,128)(2,1)} %param.10) | copy-start | bytes 294916
  7.2 73.1 %all-gather.2.cloned.1.call-start = ((), (), s32[]{:S(2)}) async-start(), calls=%async_computation.1 | async-start | bytes 2359296 | tf_op jit(solution)/shard_map/all_gather | solution.py:113
  7.3 12.4 %collective-permute-start = (bf16[1,2,2,128,128]{4,3,2,1,0:T(8,128)(2,1)}, bf16[1,2,2,128,128]{4,3,2,1,0:T(8,128)(2,1)S(1)}, u32[]{:S(2)}, u32[]{:S(2)}) collective-permute-start(bf16[1,2,2,128,128]{4,3,2,1,0:T(8,128)(2,1)} %param.9), channel_id=1, source_target_pairs={{0,1},{1,2},{2,3},{3,4},{4,5},{5,6},{6,7},{7,64},{64,65},{65,66},{... | collective-permute-start | bytes 393224 | tf_op jit(solution)/shard_map/ppermute | solution.py:11
  24.7 17.9 %all-to-all-start = ((f32[32,1,2,3,3,128]{5,2,4,3,1,0:T(2,128)}), f32[32,1,2,3,3,128]{5,2,4,3,1,0:T(2,128)S(1)}, u32[]{:S(2)}, u32[]{:S(2)}) async-start(f32[32,1,2,3,3,128]{5,2,4,3,1,0:T(2,128)} %stack.112), calls=%async_computation | async-start | bytes 589824 | tf_op jit(solution)/shard_map/all_to_all | solution.py:97
  96.4 5.8 %copy-start.2 = (f32[2,128,128]{2,1,0:T(8,128)S(1)}, f32[2,128,128]{2,1,0:T(8,128)}, u32[]{:S(2)}) copy-start(f32[2,128,128]{2,1,0:T(8,128)} %copy.253) | copy-start | bytes 393220 | tf_op jit(solution)/shard_map/while
  96.4 5.8 %copy-start.3 = (f32[2,128,128]{2,1,0:T(8,128)S(1)}, f32[2,128,128]{2,1,0:T(8,128)}, u32[]{:S(2)}) copy-start(f32[2,128,128]{2,1,0:T(8,128)} %copy.254) | copy-start | bytes 393220 | tf_op jit(solution)/shard_map/while
  96.4 5.8 %copy-start.4 = (f32[2,128,128]{2,1,0:T(8,128)S(1)}, f32[2,128,128]{2,1,0:T(8,128)}, u32[]{:S(2)}) copy-start(f32[2,128,128]{2,1,0:T(8,128)} %copy.255) | copy-start | bytes 393220 | tf_op jit(solution)/shard_map/while
  96.4 5.8 %copy-start.5 = (f32[2,128,128]{2,1,0:T(8,128)S(1)}, f32[2,128,128]{2,1,0:T(8,128)}, u32[]{:S(2)}) copy-start(f32[2,128,128]{2,1,0:T(8,128)} %copy.256) | copy-start | bytes 393220 | tf_op jit(solution)/shard_map/while
  96.5 5.8 %copy-start.6 = (f32[2,128,128]{2,1,0:T(8,128)S(1)}, f32[2,128,128]{2,1,0:T(8,128)}, u32[]{:S(2)}) copy-start(f32[2,128,128]{2,1,0:T(8,128)} %copy.257) | copy-start | bytes 393220 | tf_op jit(solution)/shard_map/while
  96.5 5.8 %copy-start.7 = (f32[2,128,128]{2,1,0:T(8,128)S(1)}, f32[2,128,128]{2,1,0:T(8,128)}, u32[]{:S(2)}) copy-start(f32[2,128,128]{2,1,0:T(8,128)} %copy.258) | copy-start | bytes 393220 | tf_op jit(solution)/shard_map/while
  125.3 5.8 %copy-start.2 = (f32[2,128,128]{2,1,0:T(8,128)S(1)}, f32[2,128,128]{2,1,0:T(8,128)}, u32[]{:S(2)}) copy-start(f32[2,128,128]{2,1,0:T(8,128)} %copy.253) | copy-start | bytes 393220 | tf_op jit(solution)/shard_map/while
  125.3 5.8 %copy-start.3 = (f32[2,128,128]{2,1,0:T(8,128)S(1)}, f32[2,128,128]{2,1,0:T(8,128)}, u32[]{:S(2)}) copy-start(f32[2,128,128]{2,1,0:T(8,128)} %copy.254) | copy-start | bytes 393220 | tf_op jit(solution)/shard_map/while
  125.3 5.8 %copy-start.4 = (f32[2,128,128]{2,1,0:T(8,128)S(1)}, f32[2,128,128]{2,1,0:T(8,128)}, u32[]{:S(2)}) copy-start(f32[2,128,128]{2,1,0:T(8,128)} %copy.255) | copy-start | bytes 393220 | tf_op jit(solution)/shard_map/while
  125.3 5.8 %copy-start.5 = (f32[2,128,128]{2,1,0:T(8,128)S(1)}, f32[2,128,128]{2,1,0:T(8,128)}, u32[]{:S(2)}) copy-start(f32[2,128,128]{2,1,0:T(8,128)} %copy.256) | copy-start | bytes 393220 | tf_op jit(solution)/shard_map/while
  125.3 5.8 %copy-start.6 = (f32[2,128,128]{2,1,0:T(8,128)S(1)}, f32[2,128,128]{2,1,0:T(8,128)}, u32[]{:S(2)}) copy-start(f32[2,128,128]{2,1,0:T(8,128)} %copy.257) | copy-start | bytes 393220 | tf_op jit(solution)/shard_map/while
  125.3 5.8 %copy-start.7 = (f32[2,128,128]{2,1,0:T(8,128)S(1)}, f32[2,128,128]{2,1,0:T(8,128)}, u32[]{:S(2)}) copy-start(f32[2,128,128]{2,1,0:T(8,128)} %copy.258) | copy-start | bytes 393220 | tf_op jit(solution)/shard_map/while
  154.4 5.8 %copy-start.2 = (f32[2,128,128]{2,1,0:T(8,128)S(1)}, f32[2,128,128]{2,1,0:T(8,128)}, u32[]{:S(2)}) copy-start(f32[2,128,128]{2,1,0:T(8,128)} %copy.253) | copy-start | bytes 393220 | tf_op jit(solution)/shard_map/while
  154.4 5.8 %copy-start.3 = (f32[2,128,128]{2,1,0:T(8,128)S(1)}, f32[2,128,128]{2,1,0:T(8,128)}, u32[]{:S(2)}) copy-start(f32[2,128,128]{2,1,0:T(8,128)} %copy.254) | copy-start | bytes 393220 | tf_op jit(solution)/shard_map/while
  154.4 5.8 %copy-start.4 = (f32[2,128,128]{2,1,0:T(8,128)S(1)}, f32[2,128,128]{2,1,0:T(8,128)}, u32[]{:S(2)}) copy-start(f32[2,128,128]{2,1,0:T(8,128)} %copy.255) | copy-start | bytes 393220 | tf_op jit(solution)/shard_map/while
  154.4 5.8 %copy-start.5 = (f32[2,128,128]{2,1,0:T(8,128)S(1)}, f32[2,128,128]{2,1,0:T(8,128)}, u32[]{:S(2)}) copy-start(f32[2,128,128]{2,1,0:T(8,128)} %copy.256) | copy-start | bytes 393220 | tf_op jit(solution)/shard_map/while
  (104 other events, 358.3 us)
Sparse Core Ops, SparseCore 0:
  21.4 58.7 all-gather.1
